TPU v7x, 32 devices: a whole 2x2x4 slice. The times are simulated.
32 devices in a mesh: groups: 2 (over x), ctx: 16 (over z, y, core).
Axes of the slice: x: 2, y: 2, z: 4, core: 2. Of those that a mesh axis runs over, the one named last changes fastest.
Arguments:
- q_latent: bfloat16 [128, 1536], P(('groups', 'ctx')), parts along dimension 0, may hold values from -64 to 64
- q_gain: float32 [1536], replicated, may hold values from 0.1 to 1.9
- w_uq: bfloat16 [1536, 24576], P(None, 'ctx'), may hold values from -0.15625 to 0.15625
- w_uk: bfloat16 [128, 128, 512], P('ctx'), may hold values from -0.5 to 0.5
- w_uv: bfloat16 [128, 512, 128], P('ctx'), may hold values from -0.25 to 0.25
- w_o: bfloat16 [16384, 7168], P('ctx'), may hold values from -0.046875 to 0.046875
- latent_cache: bfloat16 [65536, 576], P(('groups', 'ctx')), parts along dimension 0, may hold values from -1024 to 1024
- kv_scales: float32 [65536, 4], P(('groups', 'ctx')), parts along dimension 0, may hold values from 0.5 to 2
- selected: int32 [128, 32], P(('groups', 'ctx')), parts along dimension 0, may hold values from 0 to 511, as said below
- counts: int32 [128], P(('groups', 'ctx')), parts along dimension 0, may hold values from 8 to 32
Outputs:
- attn_out: bfloat16 [128, 7168], P(('groups', 'ctx')), parts along dimension 0
There are 2 independent parts, one for each index of `groups`. A program takes and returns all parts, laid end to end along the dimension named above; an argument that names none is the same for every part. Nothing has to cross between parts.
Inputs may be any that keep to these rules, and one draw needn't show every extreme that they name: `selected`: each row lists 32 different block numbers. Over the rows 4 i to 4 i + 4 - 1 (the query tokens of one device) and their first counts entries, at most 8 different listed blocks lie in the range 32 j to 32 j + 31 for any j.
All inputs are finite; a program needn't handle non-finite values.
Results may differ from a plain program's by a relative error of at most 0.01.
The roundings to bfloat16 on the way count: a program that leaves them out, or rounds other values in their place, can miss the bound.
Values may be sent and summed in bfloat16 or wider, within the bound.
A program may use at most 128 MiB of HBM per device.

v0:
```python
import math
import jax
import jax.numpy as jnp
from jax import lax
from jax.sharding import PartitionSpec as P

BLK = 64
norm_eps = 1e-06
rope_base = 10000.0


def rotate_rotary(rotary, positions):
    half_width = rotary.shape[-1] // 2
    freq_index = jnp.arange(half_width, dtype=jnp.float32)
    inverse_freq = jnp.exp(freq_index * (-2.0 * math.log(rope_base) / rotary.shape[-1]))
    angles = positions[:, None] * inverse_freq[None, :]
    cosine = jnp.cos(angles)[:, None, :]
    sine = jnp.sin(angles)[:, None, :]
    first_half = rotary[:, :, :half_width]
    second_half = rotary[:, :, half_width:]
    return jnp.concatenate(
        [first_half * cosine - second_half * sine, first_half * sine + second_half * cosine], axis=2
    )


def local(q_latent, q_gain, w_uq, w_uk, w_uv, w_o, latent_cache, kv_scales, selected, counts):
    n_devices = lax.axis_size("ctx")
    heads_local = w_uk.shape[0]
    width_content = w_uk.shape[1]
    width_latent = w_uk.shape[2]
    width_rotary = latent_cache.shape[1] - width_latent
    width_row = width_latent + width_rotary
    q_local = q_latent.shape[0]
    top_blocks = selected.shape[1]
    block_len = BLK
    blocks_local = latent_cache.shape[0] // block_len
    blocks_total = blocks_local * n_devices
    capacity = max(2, 4 * top_blocks // n_devices)
    latent_f = q_latent.astype(jnp.float32)
    normed = (
        latent_f
        * lax.rsqrt(jnp.mean(latent_f * latent_f, axis=1, keepdims=True) + norm_eps)
        * q_gain
    ).astype(jnp.bfloat16)
    scaled = (
        latent_cache[:, :width_latent].astype(jnp.float32)
        * jnp.repeat(kv_scales, width_latent // kv_scales.shape[1], axis=1)
    ).astype(jnp.bfloat16)
    cache_blocks = jnp.concatenate([scaled, latent_cache[:, width_latent:]], axis=1).reshape(
        blocks_local, block_len, width_row
    )
    live_sel = jnp.arange(top_blocks, dtype=jnp.int32)[None, :] < counts[:, None]
    block_match = selected[:, :, None] == jnp.arange(blocks_total, dtype=jnp.int32)[None, None, :]
    needed = (
        jnp.any(block_match & live_sel[:, :, None], axis=(0, 1))
        .reshape(n_devices, blocks_local)
        .astype(jnp.int32)
    )
    order_rank = jnp.cumsum(needed, axis=1) - 1
    slot_match = (needed[:, :, None] == 1) & (
        order_rank[:, :, None] == jnp.arange(capacity, dtype=jnp.int32)[None, None, :]
    )
    requests = jnp.sum(
        jnp.where(slot_match, jnp.arange(blocks_local, dtype=jnp.int32)[None, :, None], 0), axis=1
    )
    rank_flat = order_rank.reshape(blocks_total)
    sel_rank = jnp.sum(jnp.where(block_match, rank_flat[None, None, :], 0), axis=2)
    slot_index = jnp.where(live_sel, selected // blocks_local * capacity + sel_rank, 0)
    shard_piece = lax.all_gather(normed, "ctx", axis=0, tiled=True)
    row_count = shard_piece.shape[0]
    projected = jnp.dot(shard_piece, w_uq, preferred_element_type=jnp.float32).reshape(
        row_count, heads_local, width_content + width_rotary
    )
    content = projected[:, :, :width_content].astype(jnp.bfloat16)
    positions = jnp.arange(row_count, dtype=jnp.int32).astype(jnp.float32)
    rotated = rotate_rotary(projected[:, :, width_content:], positions).astype(jnp.bfloat16)
    absorbed = jnp.einsum("khn,hnc->khc", content, w_uk, preferred_element_type=jnp.float32).astype(
        jnp.bfloat16
    )
    head_queries = jnp.concatenate([absorbed, rotated], axis=2)
    queries = lax.all_to_all(head_queries, "ctx", split_axis=0, concat_axis=1, tiled=True)
    served = cache_blocks[lax.all_to_all(requests, "ctx", split_axis=0, concat_axis=0, tiled=True)]
    fetched = lax.all_to_all(served, "ctx", split_axis=0, concat_axis=0, tiled=True)
    fetched_rows = fetched.reshape(n_devices * capacity * block_len, width_row)
    token_index = (
        slot_index[:, :, None] * block_len + jnp.arange(block_len, dtype=jnp.int32)[None, None, :]
    ).reshape(q_local, top_blocks * block_len)
    live_tokens = jnp.repeat(live_sel, block_len, axis=1)
    softmax_scale = 1.0 / math.sqrt(width_content + width_rotary)

    def attend(inputs):
        query_row, token_rows, live_row = inputs
        key_rows = fetched_rows[token_rows]
        scores = jnp.dot(query_row, key_rows.T, preferred_element_type=jnp.float32) * softmax_scale
        scores = jnp.where(live_row[None, :], scores, -jnp.inf)
        row_peak = jnp.max(scores, axis=1, keepdims=True)
        exponent = jnp.exp(scores - row_peak)
        weights = (exponent / jnp.sum(exponent, axis=1, keepdims=True)).astype(jnp.bfloat16)
        return jnp.dot(
            weights, key_rows[:, :width_latent], preferred_element_type=jnp.float32
        ).astype(jnp.bfloat16)

    latent_out = lax.map(attend, (queries, token_index, live_tokens))
    head_out = lax.all_to_all(latent_out, "ctx", split_axis=1, concat_axis=0, tiled=True)
    head_values = jnp.einsum(
        "qhc,hcv->qhv", head_out, w_uv, preferred_element_type=jnp.float32
    ).astype(jnp.bfloat16)
    head_values = head_values.reshape(head_values.shape[0], heads_local * w_uv.shape[2])
    return lax.psum_scatter(
        jnp.dot(head_values, w_o, preferred_element_type=jnp.float32),
        "ctx",
        scatter_dimension=0,
        tiled=True,
    ).astype(jnp.bfloat16)


def solution(mesh):
    in_specs = (
        P(("groups", "ctx"), None),
        P(),
        P(None, "ctx"),
        P("ctx", None, None),
        P("ctx", None, None),
        P("ctx", None),
        P(("groups", "ctx"), None),
        P(("groups", "ctx"), None),
        P(("groups", "ctx"), None),
        P(("groups", "ctx")),
    )
    out_specs = P(("groups", "ctx"), None)
    return jax.shard_map(local, mesh=mesh, in_specs=in_specs, out_specs=out_specs, check_vma=False)
```

profile of v0, /device:TPU:0, one launch (start us, length us, event | category | flops | bytes accessed | tf_op | source)
XLA Modules:
  0.0 466.6 jit_solution(13454047989507777395)
XLA Ops:
  0.0 0.8 iota_compare_fusion.2
  0.8 0.8 fusion.22
  1.9 1.0 select_reduce_fusion.1
  2.9 7.4 %all-to-all-start.1 = ((s32[16,1,8]{2,1,0:T(1,128)}), s32[16,1,8]{2,1,0:T(1,128)S(1)}, u32[]{:S(2)}, u32[]{:S(2)}) async-start(s32[16,1,8]{2,1,0:T(1,128)} %bitcast.18), calls=%async_computation.1 | async-start | bytes 16384 | tf_op jit(solution)/shard_map/all_to_all | solution.py:82
  10.3 0.8 fusion.27
  11.2 0.8 fusion.30
  12.0 22.2 %all-gather = bf16[16,4,1536]{2,1,0:T(4,128)(2,1)S(1)} all-gather(bf16[1,4,1536]{2,1,0:T(4,128)(2,1)S(1)} %fusion.30), channel_id=1, replica_groups=mesh['groups'=2,'ctx'=16] {'ctx'}, dimensions={0}, use_global_device_ids=true | all-gather | bytes 208896 | tf_op jit(solution)/shard_map/all_gather | solution.py:69
  34.2 3.3 fusion.39
  38.0 0.3 fusion.19
  38.6 1.2 copy.45
  39.8 0.4 copy.48
  40.2 0.2 slice-done
  40.4 2.5 copy.59
  42.9 1.0 copy.60
  44.0 4.3 all-to-all-start
  48.2 4.7 %broadcast_in_dim.79 = f32[2048,4,128]{2,1,0:T(4,128)S(1)} broadcast(f32[2048,4]{1,0:T(8,128)S(1)} %copy.48), dimensions={0,1} | broadcast | bytes 4227072 | tf_op jit(solution)/shard_map/broadcast_in_dim | solution.py:47
  52.9 1.0 fusion.18
  54.0 0.2 pad_maximum_fusion
  54.5 7.6 %gather_fusion.1 = bf16[128,64,576]{2,1,0:T(8,128)(2,1)} fusion(bf16[32,64,576]{2,1,0:T(8,128)(2,1)S(1)} %bitcast.67, s32[1024]{0:T(1024)S(1)} %pad_clamp_fusion), kind=kCustom, calls=%fused_computation.1 | custom fusion | bytes 18874880 | tf_op jit(solution)/shard_map/gather | solution.py:82
  62.1 2.7 all-to-all-done
  64.8 5.1 %all-to-all-start.2 = ((bf16[16,8,64,576]{3,2,1,0:T(8,128)(2,1)}), bf16[16,8,64,576]{3,2,1,0:T(8,128)(2,1)}, u32[]{:S(2)}, u32[]{:S(2)}) async-start(bf16[16,8,64,576]{3,2,1,0:T(8,128)(2,1)} %bitcast.68), calls=%async_computation.2 | async-start | bytes 20971520 | tf_op jit(solution)/shard_map/all_to_all | solution.py:83
  70.8 1.1 copy.79
  72.0 184.8 %all-to-all-done.2 = bf16[16,8,64,576]{3,2,1,0:T(8,128)(2,1)} async-done(((bf16[16,8,64,576]{3,2,1,0:T(8,128)(2,1)}), bf16[16,8,64,576]{3,2,1,0:T(8,128)(2,1)}, u32[]{:S(2)}, u32[]{:S(2)}) %all-to-all-start.2) | async-done | bytes 9437216 | tf_op jit(solution)/shard_map/all_to_all | solution.py:83
  256.8 63.6 %while.10 = (s32[]{:T(128)}, bf16[4,128,512]{2,1,0:T(8,128)(2,1)}, pred[4,2048]{1,0:T(4,128)(4,1)S(1)}, bf16[4,128,576]{2,1,0:T(8,128)(2,1)S(1)}, s32[4,2048]{1,...) while((s32[]{:T(128)}, bf16[4,128,512]{2,1,0:T(8,128)(2,1)}, pred[4,2048]{1,0:T(4,128)(4,1)S(1)}, ...), condition=%wide.region_8.9_spmd, body=%wide.region_5.8_spmd.sunk | while | flops 572595968 | bytes 12928089 | solution.py:103
  256.8 13.3 %gather_fusion = bf16[2048,576]{1,0:T(8,128)(2,1)S(1)} fusion(bf16[8192,576]{1,0:T(8,128)(2,1)} %get-tuple-element.118, s32[2048]{0:T(1024)S(1)} %broadcast_clamp_fusion.2), kind=kCustom, calls=%fused_computation.clone.1 | custom fusion | bytes 4726784 | tf_op jit(solution)/shard_map/while/body/eval_jaxpr/gather | solution.py:93
  270.2 1.1 fusion.54
  271.2 0.3 fusion.55
  271.5 1.2 fusion.56
  272.8 13.3 %gather_fusion = bf16[2048,576]{1,0:T(8,128)(2,1)S(1)} fusion(bf16[8192,576]{1,0:T(8,128)(2,1)} %get-tuple-element.118, s32[2048]{0:T(1024)S(1)} %broadcast_clamp_fusion.2), kind=kCustom, calls=%fused_computation.clone.1 | custom fusion | bytes 4726784 | tf_op jit(solution)/shard_map/while/body/eval_jaxpr/gather | solution.py:93
  286.1 1.1 fusion.54
  287.2 0.3 fusion.55
  287.5 1.2 fusion.56
  288.7 13.3 %gather_fusion = bf16[2048,576]{1,0:T(8,128)(2,1)S(1)} fusion(bf16[8192,576]{1,0:T(8,128)(2,1)} %get-tuple-element.118, s32[2048]{0:T(1024)S(1)} %broadcast_clamp_fusion.2), kind=kCustom, calls=%fused_computation.clone.1 | custom fusion | bytes 4726784 | tf_op jit(solution)/shard_map/while/body/eval_jaxpr/gather | solution.py:93
  302.0 1.1 fusion.54
  303.1 0.3 fusion.55
  303.4 1.2 fusion.56
  304.6 13.3 %gather_fusion = bf16[2048,576]{1,0:T(8,128)(2,1)S(1)} fusion(bf16[8192,576]{1,0:T(8,128)(2,1)} %get-tuple-element.118, s32[2048]{0:T(1024)S(1)} %broadcast_clamp_fusion.2), kind=kCustom, calls=%fused_computation.clone.1 | custom fusion | bytes 4726784 | tf_op jit(solution)/shard_map/while/body/eval_jaxpr/gather | solution.py:93
  317.9 1.1 fusion.54
  319.0 0.3 fusion.55
  319.3 1.2 fusion.56
  320.4 2.3 copy.54
  322.8 45.6 %all-to-all-start.3 = ((bf16[4,128,512]{2,0,1:T(4,128)(2,1)}), bf16[4,128,512]{2,0,1:T(4,128)(2,1)S(1)}, u32[]{:S(2)}, u32[]{:S(2)}) async-start(bf16[4,128,512]{2,0,1:T(4,128)(2,1)} %copy.54), calls=%async_computation.3 | async-start | bytes 1048576 | tf_op jit(solution)/shard_map/all_to_all | solution.py:104
  368.4 0.6 dynamic-slice
  369.7 13.0 %all-to-all-done.3 = bf16[4,128,512]{2,0,1:T(4,128)(2,1)S(1)} async-done(((bf16[4,128,512]{2,0,1:T(4,128)(2,1)}), bf16[4,128,512]{2,0,1:T(4,128)(2,1)S(1)}, u32[]{:S(2)}, u32[]{:S(2)}) %all-to-all-start.3) | async-done | bytes 524320 | tf_op jit(solution)/shard_map/all_to_all | solution.py:104
  383.0 0.3 fusion.20
  383.3 8.0 %fusion.23 = f32[64,7168]{1,0:T(8,128)S(1)} fusion(bf16[1024,7168]{1,0:T(8,128)(2,1)} %param.17, bf16[8,8,8,128]{3,2,1,0:T(8,128)(2,1)S(1)} %fusion.20), kind=kOutput, calls=%fused_computation.37 | convolution fusion | flops 939524096 | bytes 16646144 | tf_op jit(solution)/shard_map/dot_general | solution.py:110
  391.3 73.7 %all-reduce.2 = bf16[64,7168]{1,0:T(8,128)(2,1)} all-reduce(f32[64,7168]{1,0:T(8,128)S(1)} %fusion.23), channel_id=2, replica_groups=mesh['groups'=2,'ctx'=16] {'ctx'}, use_global_device_ids=true, to_apply=%region_9.10.clone | all-reduce | flops 458752 | bytes 2752512
  465.1 1.6 dynamic-slice_convert_fusion
  (67 shorter events, 2.8 us)
Async XLA Ops:
  0.0 38.0 %copy-start = (bf16[8,128,512]{2,1,0:T(8,128)(2,1)S(1)}, bf16[8,128,512]{2,1,0:T(8,128)(2,1)}, u32[]{:S(2)}) copy-start(bf16[8,128,512]{2,1,0:T(8,128)(2,1)} %param.15) | copy-start | bytes 3145732
  2.9 41.1 %all-to-all-start.1 = ((s32[16,1,8]{2,1,0:T(1,128)}), s32[16,1,8]{2,1,0:T(1,128)S(1)}, u32[]{:S(2)}, u32[]{:S(2)}) async-start(s32[16,1,8]{2,1,0:T(1,128)} %bitcast.18), calls=%async_computation.1 | async-start | bytes 16384 | tf_op jit(solution)/shard_map/all_to_all | solution.py:82
  38.6 1.2 copy-start.5
  38.6 1.8 slice-start
  39.8 3.1 slice-start.1
  44.0 20.9 %all-to-all-start = ((bf16[64,8,576]{2,1,0:T(8,128)(2,1)}), bf16[64,8,576]{2,1,0:T(8,128)(2,1)}, u32[]{:S(2)}, u32[]{:S(2)}) async-start(bf16[64,8,576]{2,1,0:T(8,128)(2,1)} %copy.45), calls=%async_computation | async-start | bytes 1310720 | tf_op jit(solution)/shard_map/all_to_all | solution.py:81
  48.2 4.7 %copy-start.2 = (bf16[2048,512]{1,0:T(8,128)(2,1)S(1)}, bf16[2048,512]{1,0:T(8,128)(2,1)}, u32[]{:S(2)}) copy-start(bf16[2048,512]{1,0:T(8,128)(2,1)} %copy.59) | copy-start | bytes 6291460
  52.9 1.0 copy-start.3
  64.8 5.2 %copy-start.6 = (s32[4,32]{1,0:T(4,128)S(1)}, s32[4,32]{1,0:T(4,128)}, u32[]{:S(2)}) copy-start(s32[4,32]{1,0:T(4,128)} %param.20) | copy-start | bytes 1540
  64.8 5.5 %copy-start.7 = (s32[4]{0:T(128)S(1)}, s32[4]{0:T(128)}, u32[]{:S(2)}) copy-start(s32[4]{0:T(128)} %param.21) | copy-start | bytes 52
  64.8 192.0 %all-to-all-start.2 = ((bf16[16,8,64,576]{3,2,1,0:T(8,128)(2,1)}), bf16[16,8,64,576]{3,2,1,0:T(8,128)(2,1)}, u32[]{:S(2)}, u32[]{:S(2)}) async-start(bf16[16,8,64,576]{3,2,1,0:T(8,128)(2,1)} %bitcast.68), calls=%async_computation.2 | async-start | bytes 20971520 | tf_op jit(solution)/shard_map/all_to_all | solution.py:83
  256.8 111.6 %copy-start.8 = (u32[32]{0:T(128)S(1)}, u32[32]{0:T(128)}, u32[]{:S(2)}) copy-start(u32[32]{0:T(128)} %constant.72) | copy-start | bytes 388
  320.4 62.6 %copy-start.4 = (bf16[8,512,128]{2,1,0:T(8,128)(2,1)S(1)}, bf16[8,512,128]{2,1,0:T(8,128)(2,1)}, u32[]{:S(2)}) copy-start(bf16[8,512,128]{2,1,0:T(8,128)(2,1)} %param.16) | copy-start | bytes 3145732
  322.8 59.9 %all-to-all-start.3 = ((bf16[4,128,512]{2,0,1:T(4,128)(2,1)}), bf16[4,128,512]{2,0,1:T(4,128)(2,1)S(1)}, u32[]{:S(2)}, u32[]{:S(2)}) async-start(bf16[4,128,512]{2,0,1:T(4,128)(2,1)} %copy.54), calls=%async_computation.3 | async-start | bytes 1048576 | tf_op jit(solution)/shard_map/all_to_all | solution.py:104
  383.3 83.3 %copy-start.1 = (bf16[8,128,512]{2,1,0:T(8,128)(2,1)S(1)}, bf16[8,128,512]{2,1,0:T(8,128)(2,1)}, u32[]{:S(2)}) copy-start(bf16[8,128,512]{2,1,0:T(8,128)(2,1)} %param.15) | copy-start | bytes 3145732
where the time goes:
time: 468 us; the launch traced here: 467 us
  waiting for transfers between devices  201 us (43%)
  blocking collectives  95.9 us (20%)
  local copies, waits for them, and re-layouts  78.1 us (17%)
  starting transfers between devices  62.5 us (13%)
  matrix products  20.8 us (4%)
  other arithmetic  7.66 us (2%)
    all_to_all x1, waiting for transfers between devices, local(): lax.all_to_all(served, 'ctx', split_axis=0, concat_axis=0, tiled=True)  185 us
    unnamed x1, blocking collectives  73.7 us
    gather x4, local copies, waits for them, and re-layouts, attend(): key_rows = fetched_rows[token_rows]  53.1 us
    all_to_all x1, starting transfers between devices, local(): lax.all_to_all(latent_out, 'ctx', split_axis=1, concat_axis=0, tiled=True)  45.6 us
    all_gather x1, blocking collectives, local(): shard_piece = lax.all_gather(normed, 'ctx', axis=0, tiled=True)  22.2 us
    all_to_all x1, waiting for transfers between devices, local(): lax.all_to_all(latent_out, 'ctx', split_axis=1, concat_axis=0, tiled=True)  13 us
  transfers between devices with their start and end apart: 4, of which 3 were waited for; matrix products, arithmetic and copies ran while one was open for 6% of the time, Pallas kernels for 0%

commit v1 on v0

--- a/solution.py
+++ b/solution.py
@@ -7,6 +7,18 @@
 BLK = 64
 norm_eps = 1e-06
 rope_base = 10000.0
+
+
+def split_up(x, dim, size):
+    lengths = x.shape
+    pieces = x.reshape(*lengths[:dim], size, lengths[dim] // size, *lengths[dim + 1 :])
+    return jnp.moveaxis(pieces, dim, 0)
+
+
+def laid_out(pieces, dim):
+    pieces = jnp.moveaxis(pieces, 0, dim)
+    shape = pieces.shape
+    return pieces.reshape(*shape[:dim], shape[dim] * shape[dim + 1], *shape[dim + 2 :])
 
 
 def rotate_rotary(rotary, positions):
@@ -80,7 +92,15 @@
     head_queries = jnp.concatenate([absorbed, rotated], axis=2)
     queries = lax.all_to_all(head_queries, "ctx", split_axis=0, concat_axis=1, tiled=True)
     served = cache_blocks[lax.all_to_all(requests, "ctx", split_axis=0, concat_axis=0, tiled=True)]
-    fetched = lax.all_to_all(served, "ctx", split_axis=0, concat_axis=0, tiled=True)
+    size, index = (lax.axis_size("ctx"), lax.axis_index("ctx"))
+    blocks = split_up(served, 0, size)
+    out = blocks
+    for step in range(1, size):
+        target, source = ((index + step) % size, (index - step) % size)
+        sent = lax.dynamic_index_in_dim(blocks, target, 0)
+        received = lax.ppermute(sent, "ctx", [(i, (i + step) % size) for i in range(size)])
+        out = lax.dynamic_update_slice_in_dim(out, received, source, axis=0)
+    fetched = laid_out(out, 0)
     fetched_rows = fetched.reshape(n_devices * capacity * block_len, width_row)
     token_index = (
         slot_index[:, :, None] * block_len + jnp.arange(block_len, dtype=jnp.int32)[None, None, :]

time: 468 us -> 523 us (1.12)
  waiting for transfers between devices: 201 us -> 125 us
  starting transfers between devices: 62.5 us -> 131 us
  local copies, waits for them, and re-layouts: 78.1 us -> 118 us
  matrix products: 20.8 us -> 32.3 us
  other arithmetic: 7.66 us -> 15.8 us
    all_to_all x1 -> x0, waiting for transfers between devices: 185 us -> none  [local(): lax.all_to_all(served, 'ctx', split_axis=0, concat_axis=0, tiled=True)]
    ppermute x0 -> x15, waiting for transfers between devices: none -> 112 us  [local(): lax.ppermute(sent, 'ctx', [(i, (i + step) % size) for i in range(size)])]
    ppermute x0 -> x15, starting transfers between devices: none -> 107 us  [local(): lax.ppermute(sent, 'ctx', [(i, (i + step) % size) for i in range(size)])]
    all_to_all x1, starting transfers between devices: 45.6 us -> 12.5 us  [local(): lax.all_to_all(latent_out, 'ctx', split_axis=1, concat_axis=0, tiled=True)]
    dynamic_update_slice x0 -> x15, local copies, waits for them, and re-layouts: none -> 19.2 us  [local(): out = lax.dynamic_update_slice_in_dim(out, received, source, axis=0)]
    dot_general x4, matrix products: 4.26 us -> 11.3 us  [attend(): jnp.dot(query_row, key_rows.T, preferred_element_type=jnp.float32)]
    dynamic_slice x0 -> x1, local copies, waits for them, and re-layouts: none -> 6.91 us  [local(): sent = lax.dynamic_index_in_dim(blocks, target, 0)]
    gather x4, local copies, waits for them, and re-layouts: 53.1 us -> 59.6 us  [attend(): key_rows = fetched_rows[token_rows]]
  transfers between devices with their start and end apart: 4 -> 18, of which waited for: 3 -> 5; matrix products, arithmetic and copies ran while one was open for 6% -> 13% of each run, Pallas kernels for 0% -> 0%
where the time goes in v1:
time: 523 us; the launch traced here: 521 us
  starting transfers between devices  131 us (25%)
  waiting for transfers between devices  125 us (24%)
  local copies, waits for them, and re-layouts  118 us (23%)
  blocking collectives  97.5 us (19%)
  matrix products  32.3 us (6%)
  other arithmetic  15.8 us (3%)
    ppermute x15, waiting for transfers between devices, local(): lax.ppermute(sent, 'ctx', [(i, (i + step) % size) for i in range(size)])  112 us
    ppermute x15, starting transfers between devices, local(): lax.ppermute(sent, 'ctx', [(i, (i + step) % size) for i in range(size)])  107 us
    unnamed x1, blocking collectives  74 us
    gather x4, local copies, waits for them, and re-layouts, attend(): key_rows = fetched_rows[token_rows]  59.6 us
    all_gather x1, blocking collectives, local(): shard_piece = lax.all_gather(normed, 'ctx', axis=0, tiled=True)  23.4 us
    dynamic_update_slice x15, local copies, waits for them, and re-layouts, local(): out = lax.dynamic_update_slice_in_dim(out, received, source, axis=0)  19.2 us
    all_to_all x1, waiting for transfers between devices, local(): lax.all_to_all(latent_out, 'ctx', split_axis=1, concat_axis=0, tiled=True)  13 us
    all_to_all x1, starting transfers between devices, local(): lax.all_to_all(latent_out, 'ctx', split_axis=1, concat_axis=0, tiled=True)  12.5 us
  transfers between devices with their start and end apart: 18, of which 5 were waited for; matrix products, arithmetic and copies ran while one was open for 13% of the time, Pallas kernels for 0%

profile of v1, /device:TPU:0, one launch (start us, length us, event | category | flops | bytes accessed | tf_op | source)
XLA Modules:
  0.0 520.9 jit_solution(3416876795139151567)
XLA Ops:
  3.1 7.4 %all-to-all-start.1 = ((s32[16,1,8]{2,1,0:T(1,128)}), s32[16,1,8]{2,1,0:T(1,128)S(1)}, u32[]{:S(2)}, u32[]{:S(2)}) async-start(s32[16,1,8]{2,1,0:T(1,128)} %bitcast.34), calls=%async_computation.1 | async-start | bytes 16384 | tf_op jit(solution)/shard_map/all_to_all | solution.py:94
  13.5 23.4 %all-gather = bf16[16,4,1536]{2,1,0:T(4,128)(2,1)} all-gather(bf16[1,4,1536]{2,1,0:T(4,128)(2,1)S(1)} %fusion.30), channel_id=1, replica_groups=mesh['groups'=2,'ctx'=16] {'ctx'}, dimensions={0}, use_global_device_ids=true | all-gather | bytes 208896 | tf_op jit(solution)/shard_map/all_gather | solution.py:81
  37.0 1.7 reshape.230
  38.6 4.1 fusion.39
  42.7 2.0 reshape.205
  44.7 1.9 fusion.38
  47.6 2.1 copy.63
  49.7 2.5 copy.74
  52.7 5.0 broadcast_in_dim.79
  57.8 2.4 fusion.18
  60.2 1.8 pad_maximum_fusion
  64.0 3.6 all-to-all-start
  67.9 9.5 %gather_fusion.1 = bf16[128,64,576]{2,1,0:T(8,128)(2,1)} fusion(bf16[32,64,576]{2,1,0:T(8,128)(2,1)} %bitcast.101, s32[1024]{0:T(1024)S(1)} %pad_clamp_fusion), kind=kCustom, calls=%fused_computation.1 | custom fusion | bytes 18874880 | tf_op jit(solution)/shard_map/gather | solution.py:94
  77.4 6.9 %dynamic-slice_bitcast_fusion = (bf16[1,1,8,64,576]{4,3,2,0,1:T(8,128)(2,1)S(1)}, bf16[1,1,8,64,576]{4,3,2,0,1:T(8,128)(2,1)S(1)}, bf16[1,1,8,64,576]{4,3,2,0,1:...) fusion(bf16[16,8,64,576]{3,2,1,0:T(8,128)(2,1)} %bitcast.98, ...), kind=kLoop, calls=%fused_computation.29 | loop fusion | bytes 17694780 | tf_op jit(solution)/shard_map/jit(dynamic_index_in_dim)/dynamic_slice | solution.py:100
  84.8 1.7 collective-permute-start.1
  86.4 2.2 collective-permute-start.2
  91.2 12.4 %collective-permute-done = bf16[1,1,8,64,576]{4,3,2,0,1:T(8,128)(2,1)} collective-permute-done((bf16[1,1,8,64,576]{4,3,2,0,1:T(8,128)(2,1)}, bf16[1,1,8,64,576]{4,3,2,0,1:T(8,128)(2,1)}, u32[]{:S(2)}, u32[]{:S(2)}) %collective-permute-start) | collective-permute-done | bytes 589856 | tf_op jit(solution)/shard_map/ppermute | solution.py:101
  103.6 2.0 constant_dynamic-update-slice_fusion.13
  105.6 11.4 %collective-permute-start.6 = (bf16[1,1,8,64,576]{4,3,2,0,1:T(8,128)(2,1)}, bf16[1,1,8,64,576]{4,3,2,0,1:T(8,128)(2,1)S(1)}, u32[]{:S(2)}, u32[]{:S(2)}) collective-permute-start(bf16[1,1,8,64,576]{4,3,2,0,1:T(8,128)(2,1)} %get-tuple-element.59), channel_id=1, source_target_pairs={{0,7},{1,8},{2,9},{3,10},{4,11},{5,12},{6,13},{7,14},{8,15},{9,0},... | collective-permute-start | bytes 1769480 | tf_op jit(solution)/shard_map/ppermute | solution.py:101
  117.0 2.0 constant_dynamic-update-slice_fusion.12
  119.0 2.4 collective-permute-start.7
  121.4 2.1 constant_dynamic-update-slice_fusion.11
  123.7 2.0 constant_dynamic-update-slice_fusion.10
  125.7 90.9 %collective-permute-done.4 = bf16[1,1,8,64,576]{4,3,2,0,1:T(8,128)(2,1)} collective-permute-done((bf16[1,1,8,64,576]{4,3,2,0,1:T(8,128)(2,1)}, bf16[1,1,8,64,576]{4,3,2,0,1:T(8,128)(2,1)}, u32[]{:S(2)}, u32[]{:S(2)}) %collective-permute-start.4) | collective-permute-done | bytes 589856 | tf_op jit(solution)/shard_map/ppermute | solution.py:101
  216.7 2.0 constant_dynamic-update-slice_fusion.9
  218.7 15.5 %collective-permute-start.10 = (bf16[1,1,8,64,576]{4,3,2,0,1:T(8,128)(2,1)}, bf16[1,1,8,64,576]{4,3,2,0,1:T(8,128)(2,1)S(1)}, u32[]{:S(2)}, u32[]{:S(2)}) collective-permute-start(bf16[1,1,8,64,576]{4,3,2,0,1:T(8,128)(2,1)} %get-tuple-element.55), channel_id=1, source_target_pairs={{0,11},{1,12},{2,13},{3,14},{4,15},{5,0},{6,1},{7,2},{8,3},{9,4},{... | collective-permute-start | bytes 1769480 | tf_op jit(solution)/shard_map/ppermute | solution.py:101
  235.1 31.6 %collective-permute-start.11 = (bf16[1,1,8,64,576]{4,3,2,0,1:T(8,128)(2,1)}, bf16[1,1,8,64,576]{4,3,2,0,1:T(8,128)(2,1)S(1)}, u32[]{:S(2)}, u32[]{:S(2)}) collective-permute-start(bf16[1,1,8,64,576]{4,3,2,0,1:T(8,128)(2,1)} %get-tuple-element.54), channel_id=1, source_target_pairs={{0,12},{1,13},{2,14},{3,15},{4,0},{5,1},{6,2},{7,3},{8,4},{9,5},{1... | collective-permute-start | bytes 1769480 | tf_op jit(solution)/shard_map/ppermute | solution.py:101
  269.7 20.7 %collective-permute-start.13 = (bf16[1,1,8,64,576]{4,3,2,0,1:T(8,128)(2,1)S(1)}, bf16[1,1,8,64,576]{4,3,2,0,1:T(8,128)(2,1)S(1)}, u32[]{:S(2)}, u32[]{:S(2)}) collective-permute-start(bf16[1,1,8,64,576]{4,3,2,0,1:T(8,128)(2,1)S(1)} %get-tuple-element.66), channel_id=1, source_target_pairs={{0,14},{1,15},{2,0},{3,1},{4,2},{5,3},{6,4},{7,5},{8,6},{9,7},{10,... | collective-permute-start | bytes 1769480 | tf_op jit(solution)/shard_map/ppermute | solution.py:101
  291.3 18.8 %collective-permute-start.14 = (bf16[1,1,8,64,576]{4,3,2,0,1:T(8,128)(2,1)S(1)}, bf16[1,1,8,64,576]{4,3,2,0,1:T(8,128)(2,1)S(1)}, u32[]{:S(2)}, u32[]{:S(2)}) collective-permute-start(bf16[1,1,8,64,576]{4,3,2,0,1:T(8,128)(2,1)S(1)} %get-tuple-element.52), channel_id=1, source_target_pairs={{0,15},{1,0},{2,1},{3,2},{4,3},{5,4},{6,5},{7,6},{8,7},{9,8},{10,9... | collective-permute-start | bytes 1769480 | tf_op jit(solution)/shard_map/ppermute | solution.py:101
  313.7 4.6 collective-permute-done.13
  319.2 4.5 collective-permute-done.14
  324.7 84.0 %while.10 = (s32[]{:T(128)}, bf16[4,128,512]{2,1,0:T(8,128)(2,1)S(1)}, pred[4,2048]{1,0:T(4,128)(4,1)S(1)}, bf16[4,128,576]{2,1,0:T(8,128)(2,1)S(1)}, s32[4,2048...) while((s32[]{:T(128)}, bf16[4,128,512]{2,1,0:T(8,128)(2,1)S(1)}, pred[4,2048]{1,0:T(4,128)(4,1)S(1)}, ...), condition=%wide.region_8.9_spmd, body=%wide.region_5.8_spmd.sunk | while | flops 572595968 | bytes 12665945 | solution.py:123
  325.6 14.9 %gather_fusion = bf16[2048,576]{1,0:T(8,128)(2,1)} fusion(bf16[8192,576]{1,0:T(8,128)(2,1)} %get-tuple-element.133, s32[2048]{0:T(1024)S(1)} %broadcast_clamp_fusion.2), kind=kCustom, calls=%fused_computation.clone.1 | custom fusion | bytes 4726784 | tf_op jit(solution)/shard_map/while/body/eval_jaxpr/gather | solution.py:113
  340.6 2.8 fusion.54
  343.7 2.1 fusion.56
  346.6 14.9 %gather_fusion = bf16[2048,576]{1,0:T(8,128)(2,1)} fusion(bf16[8192,576]{1,0:T(8,128)(2,1)} %get-tuple-element.133, s32[2048]{0:T(1024)S(1)} %broadcast_clamp_fusion.2), kind=kCustom, calls=%fused_computation.clone.1 | custom fusion | bytes 4726784 | tf_op jit(solution)/shard_map/while/body/eval_jaxpr/gather | solution.py:113
  361.5 2.8 fusion.54
  364.7 2.1 fusion.56
  367.6 14.9 %gather_fusion = bf16[2048,576]{1,0:T(8,128)(2,1)} fusion(bf16[8192,576]{1,0:T(8,128)(2,1)} %get-tuple-element.133, s32[2048]{0:T(1024)S(1)} %broadcast_clamp_fusion.2), kind=kCustom, calls=%fused_computation.clone.1 | custom fusion | bytes 4726784 | tf_op jit(solution)/shard_map/while/body/eval_jaxpr/gather | solution.py:113
  382.5 2.8 fusion.54
  385.6 2.1 fusion.56
  388.6 14.9 %gather_fusion = bf16[2048,576]{1,0:T(8,128)(2,1)} fusion(bf16[8192,576]{1,0:T(8,128)(2,1)} %get-tuple-element.133, s32[2048]{0:T(1024)S(1)} %broadcast_clamp_fusion.2), kind=kCustom, calls=%fused_computation.clone.1 | custom fusion | bytes 4726784 | tf_op jit(solution)/shard_map/while/body/eval_jaxpr/gather | solution.py:113
  403.5 2.8 fusion.54
  406.6 2.1 fusion.56
  409.9 12.5 %all-to-all-start.2 = ((bf16[4,128,512]{2,0,1:T(4,128)(2,1)}), bf16[4,128,512]{2,0,1:T(4,128)(2,1)S(1)}, u32[]{:S(2)}, u32[]{:S(2)}) async-start(bf16[4,128,512]{2,0,1:T(4,128)(2,1)} %copy.69), calls=%async_computation.2 | async-start | bytes 1048576 | tf_op jit(solution)/shard_map/all_to_all | solution.py:124
  423.7 13.0 %all-to-all-done.2 = bf16[4,128,512]{2,0,1:T(4,128)(2,1)S(1)} async-done(((bf16[4,128,512]{2,0,1:T(4,128)(2,1)}), bf16[4,128,512]{2,0,1:T(4,128)(2,1)S(1)}, u32[]{:S(2)}, u32[]{:S(2)}) %all-to-all-start.2) | async-done | bytes 524320 | tf_op jit(solution)/shard_map/all_to_all | solution.py:124
  437.4 7.9 %fusion.23 = f32[64,7168]{1,0:T(8,128)S(1)} fusion(bf16[1024,7168]{1,0:T(8,128)(2,1)} %param.17, bf16[8,8,8,128]{3,2,1,0:T(8,128)(2,1)S(1)} %fusion.20), kind=kOutput, calls=%fused_computation.52 | convolution fusion | flops 939524096 | bytes 16646144 | tf_op jit(solution)/shard_map/dot_general | solution.py:130
  445.3 74.0 %all-reduce.2 = bf16[64,7168]{1,0:T(8,128)(2,1)} all-reduce(f32[64,7168]{1,0:T(8,128)S(1)} %fusion.23), channel_id=2, replica_groups=mesh['groups'=2,'ctx'=16] {'ctx'}, use_global_device_ids=true, to_apply=%region_9.10.clone | all-reduce | flops 458752 | bytes 2752512
  (117 shorter events, 31.5 us)
Async XLA Ops:
  0.0 62.2 %copy-start = (bf16[8,128,512]{2,1,0:T(8,128)(2,1)S(1)}, bf16[8,128,512]{2,1,0:T(8,128)(2,1)}, u32[]{:S(2)}) copy-start(bf16[8,128,512]{2,1,0:T(8,128)(2,1)} %param.15) | copy-start | bytes 3145732
  0.0 52.5 %copy-start.5 = (s32[4,32]{1,0:T(4,128)S(1)}, s32[4,32]{1,0:T(4,128)}, u32[]{:S(2)}) copy-start(s32[4,32]{1,0:T(4,128)} %param.20) | copy-start | bytes 1540
  0.0 49.7 %slice-start = ((bf16[2048,576]{0,1:T(8,128)(2,1)}), bf16[2048,512]{0,1:T(8,128)(2,1)S(1)}, s32[]{:S(2)}) async-start(bf16[2048,576]{0,1:T(8,128)(2,1)} %param.18), calls=%async_computation.3 | async-start | bytes 4194304 | tf_op jit(solution)/shard_map/slice | solution.py:58
  0.0 52.2 %slice-start.1 = ((bf16[2048,576]{0,1:T(8,128)(2,1)}), bf16[2048,64]{0,1:T(8,128)(2,1)S(1)}, s32[]{:S(2)}) async-start(bf16[2048,576]{0,1:T(8,128)(2,1)} %param.18), calls=%async_computation.4 | async-start | bytes 524288 | tf_op jit(solution)/shard_map/slice | solution.py:61
  0.9 1.0 copy-start.6
  3.1 60.9 %all-to-all-start.1 = ((s32[16,1,8]{2,1,0:T(1,128)}), s32[16,1,8]{2,1,0:T(1,128)S(1)}, u32[]{:S(2)}, u32[]{:S(2)}) async-start(s32[16,1,8]{2,1,0:T(1,128)} %bitcast.34), calls=%async_computation.1 | async-start | bytes 16384 | tf_op jit(solution)/shard_map/all_to_all | solution.py:94
  52.2 9.8 %copy-start.8 = (f32[64]{0:T(128)S(1)}, f32[64]{0:T(128)}, u32[]{:S(2)}) copy-start(f32[64]{0:T(128)} %iota_convert_fusion) | copy-start | bytes 772
  52.2 9.8 %copy-start.9 = (f32[32]{0:T(128)S(1)}, f32[32]{0:T(128)}, u32[]{:S(2)}) copy-start(f32[32]{0:T(128)} %multiply_exponential_fusion) | copy-start | bytes 388
  52.5 10.0 %copy-start.3 = (f32[64,8,32]{2,1,0:T(8,128)S(1)}, f32[64,8,32]{2,1,0:T(8,128)}, u32[]{:S(2)}) copy-start(f32[64,8,32]{2,1,0:T(8,128)} %get-tuple-element.69) | copy-start | bytes 196612
  52.5 10.0 %copy-start.4 = (f32[64,8,32]{2,1,0:T(8,128)S(1)}, f32[64,8,32]{2,1,0:T(8,128)}, u32[]{:S(2)}) copy-start(f32[64,8,32]{2,1,0:T(8,128)} %get-tuple-element.70) | copy-start | bytes 196612
  64.0 260.6 %all-to-all-start = ((bf16[64,8,576]{2,1,0:T(8,128)(2,1)}), bf16[64,8,576]{2,1,0:T(8,128)(2,1)S(1)}, u32[]{:S(2)}, u32[]{:S(2)}) async-start(bf16[64,8,576]{2,1,0:T(8,128)(2,1)} %copy.60), calls=%async_computation | async-start | bytes 1310720 | tf_op jit(solution)/shard_map/all_to_all | solution.py:93
  77.4 7.0 %copy-start.10 = (s32[4]{0:T(128)S(1)}, s32[4]{0:T(128)}, u32[]{:S(2)}) copy-start(s32[4]{0:T(128)} %param.21) | copy-start | bytes 52
  77.4 13.5 %copy-start.7 = (pred[4,32]{1,0:T(4,128)(4,1)S(1)}, pred[4,32]{1,0:T(4,128)(4,1)}, u32[]{:S(2)}) copy-start(pred[4,32]{1,0:T(4,128)(4,1)} %copy-done.6) | copy-start | bytes 388
  84.3 19.2 %collective-permute-start = (bf16[1,1,8,64,576]{4,3,2,0,1:T(8,128)(2,1)}, bf16[1,1,8,64,576]{4,3,2,0,1:T(8,128)(2,1)}, u32[]{:S(2)}, u32[]{:S(2)}) collective-permute-start(bf16[1,1,8,64,576]{4,3,2,0,1:T(8,128)(2,1)} %get-tuple-element.65), channel_id=1, source_target_pairs={{0,1},{1,2},{2,3},{3,4},{4,5},{5,6},{6,7},{7,8},{8,9},{9,10},{10,1... | collective-permute-start | bytes 1769480 | tf_op jit(solution)/shard_map/ppermute | solution.py:101
  84.8 20.8 %collective-permute-start.1 = (bf16[1,1,8,64,576]{4,3,2,0,1:T(8,128)(2,1)}, bf16[1,1,8,64,576]{4,3,2,0,1:T(8,128)(2,1)}, u32[]{:S(2)}, u32[]{:S(2)}) collective-permute-start(bf16[1,1,8,64,576]{4,3,2,0,1:T(8,128)(2,1)} %get-tuple-element.64), channel_id=1, source_target_pairs={{0,2},{1,3},{2,4},{3,5},{4,6},{5,7},{6,8},{7,9},{8,10},{9,11},{10,... | collective-permute-start | bytes 1769480 | tf_op jit(solution)/shard_map/ppermute | solution.py:101
  86.4 32.6 %collective-permute-start.2 = (bf16[1,1,8,64,576]{4,3,2,0,1:T(8,128)(2,1)}, bf16[1,1,8,64,576]{4,3,2,0,1:T(8,128)(2,1)}, u32[]{:S(2)}, u32[]{:S(2)}) collective-permute-start(bf16[1,1,8,64,576]{4,3,2,0,1:T(8,128)(2,1)} %get-tuple-element.63), channel_id=1, source_target_pairs={{0,3},{1,4},{2,5},{3,6},{4,7},{5,8},{6,9},{7,10},{8,11},{9,12},{10... | collective-permute-start | bytes 1769480 | tf_op jit(solution)/shard_map/ppermute | solution.py:101
  88.7 34.8 %collective-permute-start.3 = (bf16[1,1,8,64,576]{4,3,2,0,1:T(8,128)(2,1)}, bf16[1,1,8,64,576]{4,3,2,0,1:T(8,128)(2,1)}, u32[]{:S(2)}, u32[]{:S(2)}) collective-permute-start(bf16[1,1,8,64,576]{4,3,2,0,1:T(8,128)(2,1)} %get-tuple-element.62), channel_id=1, source_target_pairs={{0,4},{1,5},{2,6},{3,7},{4,8},{5,9},{6,10},{7,11},{8,12},{9,13},{1... | collective-permute-start | bytes 1769480 | tf_op jit(solution)/shard_map/ppermute | solution.py:101
  90.1 126.6 %collective-permute-start.4 = (bf16[1,1,8,64,576]{4,3,2,0,1:T(8,128)(2,1)}, bf16[1,1,8,64,576]{4,3,2,0,1:T(8,128)(2,1)}, u32[]{:S(2)}, u32[]{:S(2)}) collective-permute-start(bf16[1,1,8,64,576]{4,3,2,0,1:T(8,128)(2,1)} %get-tuple-element.61), channel_id=1, source_target_pairs={{0,5},{1,6},{2,7},{3,8},{4,9},{5,10},{6,11},{7,12},{8,13},{9,14},{... | collective-permute-start | bytes 1769480 | tf_op jit(solution)/shard_map/ppermute | solution.py:101
  103.6 115.1 %collective-permute-start.5 = (bf16[1,1,8,64,576]{4,3,2,0,1:T(8,128)(2,1)}, bf16[1,1,8,64,576]{4,3,2,0,1:T(8,128)(2,1)S(1)}, u32[]{:S(2)}, u32[]{:S(2)}) collective-permute-start(bf16[1,1,8,64,576]{4,3,2,0,1:T(8,128)(2,1)} %get-tuple-element.60), channel_id=1, source_target_pairs={{0,6},{1,7},{2,8},{3,9},{4,10},{5,11},{6,12},{7,13},{8,14},{9,15},... | collective-permute-start | bytes 1769480 | tf_op jit(solution)/shard_map/ppermute | solution.py:101
  105.6 129.5 %collective-permute-start.6 = (bf16[1,1,8,64,576]{4,3,2,0,1:T(8,128)(2,1)}, bf16[1,1,8,64,576]{4,3,2,0,1:T(8,128)(2,1)S(1)}, u32[]{:S(2)}, u32[]{:S(2)}) collective-permute-start(bf16[1,1,8,64,576]{4,3,2,0,1:T(8,128)(2,1)} %get-tuple-element.59), channel_id=1, source_target_pairs={{0,7},{1,8},{2,9},{3,10},{4,11},{5,12},{6,13},{7,14},{8,15},{9,0},... | collective-permute-start | bytes 1769480 | tf_op jit(solution)/shard_map/ppermute | solution.py:101
  119.0 148.6 %collective-permute-start.7 = (bf16[1,1,8,64,576]{4,3,2,0,1:T(8,128)(2,1)}, bf16[1,1,8,64,576]{4,3,2,0,1:T(8,128)(2,1)S(1)}, u32[]{:S(2)}, u32[]{:S(2)}) collective-permute-start(bf16[1,1,8,64,576]{4,3,2,0,1:T(8,128)(2,1)} %get-tuple-element.58), channel_id=1, source_target_pairs={{0,8},{1,9},{2,10},{3,11},{4,12},{5,13},{6,14},{7,15},{8,0},{9,1},... | collective-permute-start | bytes 1769480 | tf_op jit(solution)/shard_map/ppermute | solution.py:101
  123.5 146.3 %collective-permute-start.8 = (bf16[1,1,8,64,576]{4,3,2,0,1:T(8,128)(2,1)}, bf16[1,1,8,64,576]{4,3,2,0,1:T(8,128)(2,1)S(1)}, u32[]{:S(2)}, u32[]{:S(2)}) collective-permute-start(bf16[1,1,8,64,576]{4,3,2,0,1:T(8,128)(2,1)} %get-tuple-element.57), channel_id=1, source_target_pairs={{0,9},{1,10},{2,11},{3,12},{4,13},{5,14},{6,15},{7,0},{8,1},{9,2},... | collective-permute-start | bytes 1769480 | tf_op jit(solution)/shard_map/ppermute | solution.py:101
  216.7 74.7 %collective-permute-start.9 = (bf16[1,1,8,64,576]{4,3,2,0,1:T(8,128)(2,1)}, bf16[1,1,8,64,576]{4,3,2,0,1:T(8,128)(2,1)S(1)}, u32[]{:S(2)}, u32[]{:S(2)}) collective-permute-start(bf16[1,1,8,64,576]{4,3,2,0,1:T(8,128)(2,1)} %get-tuple-element.56), channel_id=1, source_target_pairs={{0,10},{1,11},{2,12},{3,13},{4,14},{5,15},{6,0},{7,1},{8,2},{9,3},... | collective-permute-start | bytes 1769480 | tf_op jit(solution)/shard_map/ppermute | solution.py:101
  218.7 92.3 %collective-permute-start.10 = (bf16[1,1,8,64,576]{4,3,2,0,1:T(8,128)(2,1)}, bf16[1,1,8,64,576]{4,3,2,0,1:T(8,128)(2,1)S(1)}, u32[]{:S(2)}, u32[]{:S(2)}) collective-permute-start(bf16[1,1,8,64,576]{4,3,2,0,1:T(8,128)(2,1)} %get-tuple-element.55), channel_id=1, source_target_pairs={{0,11},{1,12},{2,13},{3,14},{4,15},{5,0},{6,1},{7,2},{8,3},{9,4},{... | collective-permute-start | bytes 1769480 | tf_op jit(solution)/shard_map/ppermute | solution.py:101
  235.1 76.8 %collective-permute-start.11 = (bf16[1,1,8,64,576]{4,3,2,0,1:T(8,128)(2,1)}, bf16[1,1,8,64,576]{4,3,2,0,1:T(8,128)(2,1)S(1)}, u32[]{:S(2)}, u32[]{:S(2)}) collective-permute-start(bf16[1,1,8,64,576]{4,3,2,0,1:T(8,128)(2,1)} %get-tuple-element.54), channel_id=1, source_target_pairs={{0,12},{1,13},{2,14},{3,15},{4,0},{5,1},{6,2},{7,3},{8,4},{9,5},{1... | collective-permute-start | bytes 1769480 | tf_op jit(solution)/shard_map/ppermute | solution.py:101
  267.6 45.2 %collective-permute-start.12 = (bf16[1,1,8,64,576]{4,3,2,0,1:T(8,128)(2,1)S(1)}, bf16[1,1,8,64,576]{4,3,2,0,1:T(8,128)(2,1)S(1)}, u32[]{:S(2)}, u32[]{:S(2)}) collective-permute-start(bf16[1,1,8,64,576]{4,3,2,0,1:T(8,128)(2,1)S(1)} %get-tuple-element.53), channel_id=1, source_target_pairs={{0,13},{1,14},{2,15},{3,0},{4,1},{5,2},{6,3},{7,4},{8,5},{9,6},{10... | collective-permute-start | bytes 1769480 | tf_op jit(solution)/shard_map/ppermute | solution.py:101
  269.7 48.6 %collective-permute-start.13 = (bf16[1,1,8,64,576]{4,3,2,0,1:T(8,128)(2,1)S(1)}, bf16[1,1,8,64,576]{4,3,2,0,1:T(8,128)(2,1)S(1)}, u32[]{:S(2)}, u32[]{:S(2)}) collective-permute-start(bf16[1,1,8,64,576]{4,3,2,0,1:T(8,128)(2,1)S(1)} %get-tuple-element.66), channel_id=1, source_target_pairs={{0,14},{1,15},{2,0},{3,1},{4,2},{5,3},{6,4},{7,5},{8,6},{9,7},{10,... | collective-permute-start | bytes 1769480 | tf_op jit(solution)/shard_map/ppermute | solution.py:101
  291.3 32.4 %collective-permute-start.14 = (bf16[1,1,8,64,576]{4,3,2,0,1:T(8,128)(2,1)S(1)}, bf16[1,1,8,64,576]{4,3,2,0,1:T(8,128)(2,1)S(1)}, u32[]{:S(2)}, u32[]{:S(2)}) collective-permute-start(bf16[1,1,8,64,576]{4,3,2,0,1:T(8,128)(2,1)S(1)} %get-tuple-element.52), channel_id=1, source_target_pairs={{0,15},{1,0},{2,1},{3,2},{4,3},{5,4},{6,5},{7,6},{8,7},{9,8},{10,9... | collective-permute-start | bytes 1769480 | tf_op jit(solution)/shard_map/ppermute | solution.py:101
  324.7 97.7 %copy-start.11 = (u32[32]{0:T(128)S(1)}, u32[32]{0:T(128)}, u32[]{:S(2)}) copy-start(u32[32]{0:T(128)} %constant.291) | copy-start | bytes 388
  324.7 112.3 %copy-start.2 = (bf16[8,512,128]{2,1,0:T(8,128)(2,1)S(1)}, bf16[8,512,128]{2,1,0:T(8,128)(2,1)}, u32[]{:S(2)}) copy-start(bf16[8,512,128]{2,1,0:T(8,128)(2,1)} %param.16) | copy-start | bytes 3145732
  409.9 26.8 %all-to-all-start.2 = ((bf16[4,128,512]{2,0,1:T(4,128)(2,1)}), bf16[4,128,512]{2,0,1:T(4,128)(2,1)S(1)}, u32[]{:S(2)}, u32[]{:S(2)}) async-start(bf16[4,128,512]{2,0,1:T(4,128)(2,1)} %copy.69), calls=%async_computation.2 | async-start | bytes 1048576 | tf_op jit(solution)/shard_map/all_to_all | solution.py:124
  437.0 83.8 %copy-start.1 = (bf16[8,128,512]{2,1,0:T(8,128)(2,1)S(1)}, bf16[8,128,512]{2,1,0:T(8,128)(2,1)}, u32[]{:S(2)}) copy-start(bf16[8,128,512]{2,1,0:T(8,128)(2,1)} %param.15) | copy-start | bytes 3145732
